TPU v7x, 32 devices: a whole 2x2x4 slice. The times are simulated.
32 devices in a mesh: dp: 8 (over z, y), fsdp: 4 (over x, core).
Axes of the slice: x: 2, y: 2, z: 4, core: 2. Of those that a mesh axis runs over, the one named last changes fastest.
Arguments:
- keys: bfloat16 [256, 8, 896], P(('dp', 'fsdp')), may hold values from -8 to 8
- residual: bfloat16 [256, 8, 896], P(('dp', 'fsdp')), may hold values from -6 to 6
- se_reduce: bfloat16 [896, 224], P('fsdp'), may hold values from -0.625 to 0.625
- se_expand: bfloat16 [896, 224], P('fsdp'), may hold values from -1.25 to 1.25
- conv_weight: bfloat16 [3, 896, 896], P(None, 'fsdp'), may hold values from -0.1875 to 0.1875
- bn_gain: float32 [896], replicated, may hold values from 0.1 to 1.9
- bn_bias: float32 [896], replicated, may hold values from -3 to 3
- shuffle: int32 [256], P(('dp', 'fsdp')), may hold values from 0 to 63, as said below
- unshuffle: int32 [256], P(('dp', 'fsdp')), may hold values from 0 to 63, as said below
Outputs:
- encoded: bfloat16 [256, 8, 896], P(('dp', 'fsdp'))
Inputs may be any that keep to these rules, and one draw needn't show every extreme that they name: `shuffle`: A permutation of the 64 positions within each group of devices sharing an fsdp index (positions ordered by dp index, then by image); each device sends exactly 1 of its images to every device of its group. `unshuffle`: the inverse of shuffle within each group.
All inputs are finite; a program needn't handle non-finite values.
Results may differ from a plain program's by a relative error of at most 0.013.
Values may be sent and summed in bfloat16 or wider, within the bound.
A program may use at most 64 MiB of HBM per device.

v0:
```python
import jax
import jax.numpy as jnp
from jax import lax
from jax.sharding import PartitionSpec as P

epsilon = 1e-05


def project_rows(flat, weight_rows):
    return jnp.dot(
        flat,
        lax.all_gather(weight_rows, "fsdp", axis=0, tiled=True),
        preferred_element_type=jnp.float32,
    )


def encode_block(batch_block, reduce_full, expand_full, conv_weight):
    images, positions, channels = batch_block.shape
    layers = conv_weight.shape[0]
    flat = batch_block.reshape(images * positions, channels)
    for layer in range(layers - 1):
        flat = jax.nn.relu(project_rows(flat, conv_weight[layer])).astype(jnp.bfloat16)
    entry = flat.reshape(images, positions, channels)
    pooled = jnp.mean(entry, axis=1, dtype=jnp.float32).astype(jnp.bfloat16)
    squeeze_act = jax.nn.relu(
        jnp.dot(pooled, reduce_full, preferred_element_type=jnp.float32)
    ).astype(jnp.bfloat16)
    excite = jax.nn.sigmoid(
        lax.dot_general(
            squeeze_act, expand_full, (((1,), (1,)), ((), ())), preferred_element_type=jnp.float32
        )
    )
    scaled = (entry * excite[:, None, :]).astype(jnp.bfloat16).reshape(images * positions, channels)
    projected = project_rows(scaled, conv_weight[layers - 1])
    return projected.reshape(images, positions, channels)


def local(keys, residual, se_reduce, se_expand, conv_weight, bn_gain, bn_bias, shuffle, unshuffle):
    images, positions, channels = keys.shape
    count = images * positions
    reduce_full, expand_full = (
        lax.all_gather(se_reduce, "fsdp", axis=0, tiled=True),
        lax.all_gather(se_expand, "fsdp", axis=0, tiled=True),
    )
    send_order = jnp.argsort(shuffle)
    back_order = jnp.argsort(send_order)
    outgoing = jnp.take(keys, send_order, axis=0)
    arrived = lax.all_to_all(outgoing, "dp", split_axis=0, concat_axis=0, tiled=True)
    projected = encode_block(arrived, reduce_full, expand_full, conv_weight)
    row_sums = jnp.sum(projected, axis=(0, 1))
    square_sums = jnp.sum(projected * projected, axis=(0, 1))
    mean_rows = row_sums / count
    variance = square_sums / count - mean_rows * mean_rows
    scale_rows = lax.rsqrt(variance + epsilon) * bn_gain
    normed_here = ((projected - mean_rows) * scale_rows + bn_bias).astype(jnp.bfloat16)
    returned = lax.all_to_all(normed_here, "dp", split_axis=0, concat_axis=0, tiled=True)
    normed = jnp.take(returned, back_order, axis=0)
    encoded = jax.nn.relu(normed.astype(jnp.float32) + residual.astype(jnp.float32))
    return encoded.astype(jnp.bfloat16)


def solution(mesh):
    placed = (
        P(("dp", "fsdp"), None, None),
        P(("dp", "fsdp"), None, None),
        P("fsdp", None),
        P("fsdp", None),
        P(None, "fsdp", None),
        P(),
        P(),
        P(("dp", "fsdp")),
        P(("dp", "fsdp")),
    )
    return jax.shard_map(
        local, mesh=mesh, in_specs=placed, out_specs=P(("dp", "fsdp"), None, None), check_vma=False
    )
```

profile of v0, /device:TPU:0, one launch (start us, length us, event | category | flops | bytes accessed | tf_op | source)
XLA Modules:
  0.0 100.1 jit_solution(3672770266905854364)
XLA Ops:
  6.5 2.4 %fusion.42 = (bf16[1,224,896]{2,1,0:T(8,128)(2,1)}, bf16[1,224,896]{2,1,0:T(8,128)(2,1)}, bf16[1,224,896]{2,1,0:T(8,128)(2,1)}) fusion(bf16[3,224,896]{2,1,0:T(8,128)(2,1)} %param.15), kind=kLoop, calls=%fused_computation.45 | loop fusion | bytes 2408448 | tf_op jit(solution)/shard_map/slice | solution.py:22
  8.9 0.0 all-gather.7.cloned.1.call-update
  9.0 0.0 all-gather.9.cloned.1.call-start
  9.0 0.7 all-gather.9.cloned.1.call-update
  9.7 0.0 all-gather.11.cloned.1.call-start
  9.8 0.7 all-gather.11.cloned.1.call-update
  10.5 1.0 sort.31
  11.5 0.6 gather_fusion
  12.0 0.7 broadcast_select_fusion
  12.8 7.3 %all-to-all-start = ((bf16[8,8,896]{2,1,0:T(8,128)(2,1)}), bf16[8,8,896]{2,1,0:T(8,128)(2,1)S(1)}, u32[]{:S(2)}, u32[]{:S(2)}) async-start(bf16[8,8,896]{2,1,0:T(8,128)(2,1)} %broadcast_select_fusion), calls=%async_computation | async-start | bytes 229376 | tf_op jit(solution)/shard_map/all_to_all | solution.py:48
  20.1 1.0 sort.32
  21.1 9.7 %all_gather.17 = bf16[896,224]{1,0:T(8,128)(2,1)S(1)} all-gather(bf16[224,224]{1,0:T(8,128)(2,1)S(1)} %copy-done.1), channel_id=1, replica_groups=mesh['dp'=8,'fsdp'=4] {'fsdp'}, dimensions={0}, use_global_device_ids=true | all-gather | bytes 501760 | tf_op jit(solution)/shard_map/all_gather | solution.py:42
  30.8 6.9 %all_gather.18 = bf16[896,224]{1,0:T(8,128)(2,1)S(1)} all-gather(bf16[224,224]{1,0:T(8,128)(2,1)S(1)} %copy-done.2), channel_id=1, replica_groups=mesh['dp'=8,'fsdp'=4] {'fsdp'}, dimensions={0}, use_global_device_ids=true | all-gather | bytes 501760 | tf_op jit(solution)/shard_map/all_gather | solution.py:43
  37.7 17.8 %all-gather.9.cloned.1.call-done = bf16[1,896,896]{2,1,0:T(8,128)(2,1)} async-done(((bf16[1,224,896]{2,1,0:T(8,128)(2,1)}), bf16[1,896,896]{2,1,0:T(8,128)(2,1)}) %all-gather.9.cloned.1.call-update) | async-done | bytes 1605648 | tf_op jit(solution)/shard_map/all_gather | solution.py:12
  55.6 2.6 %bitcast_reduce_fusion = (f32[8,896]{1,0:T(8,128)S(1)}, f32[64,896]{1,0:T(8,128)S(1)}) fusion(bf16[1,896,896]{2,1,0:T(8,128)(2,1)} %all-gather.9.cloned.1.call-done, bf16[1,896,896]{2,1,0:T(8,128)(2,1)} %all-gather.7.cloned.1.call-done, bf16[8,8,896]{2,1,0:T(8,128)(2,1)S(1)} %all-to-all-done), kind=kOutput, calls=%fused_computation.21 | convolution fusion | flops 205857792 | bytes 3584000 | tf_op jit(solution)/shard_map/dot_general | solution.py:10
  58.2 0.0 copy-start.4
  58.2 0.4 fusion.25
  58.6 18.4 %all-gather.11.cloned.1.call-done = bf16[1,896,896]{2,1,0:T(8,128)(2,1)} async-done(((bf16[1,224,896]{2,1,0:T(8,128)(2,1)}), bf16[1,896,896]{2,1,0:T(8,128)(2,1)}) %all-gather.11.cloned.1.call-update) | async-done | bytes 1605648 | tf_op jit(solution)/shard_map/all_gather | solution.py:12
  77.0 1.8 %fusion.41 = (f32[896]{0:T(1024)S(1)}, f32[896]{0:T(1024)S(1)}, f32[8,8,896]{2,1,0:T(8,128)S(1)}) fusion(bf16[1,896,896]{2,1,0:T(8,128)(2,1)} %all-gather.11.cloned.1.call-done, f32[64,896]{1,0:T(8,128)S(1)} %get-tuple-element.18, f32[8,896]{1,0:T(8,128)S(1)} %fusion.25), kind=kOutput, calls=%fused_computation.44 | convolution fusion | flops 103045376 | bytes 2100224 | tf_op jit(solution)/shard_map/dot_general | solution.py:10
  78.8 0.7 add_convert_fusion
  79.5 5.5 %all-to-all-start.1 = ((bf16[8,8,896]{2,1,0:T(8,128)(2,1)}), bf16[8,8,896]{2,1,0:T(8,128)(2,1)S(1)}, u32[]{:S(2)}, u32[]{:S(2)}) async-start(bf16[8,8,896]{2,1,0:T(8,128)(2,1)} %add_convert_fusion), calls=%async_computation.1 | async-start | bytes 229376 | tf_op jit(solution)/shard_map/all_to_all | solution.py:56
  85.0 7.2 %all-to-all-done.1 = bf16[8,8,896]{2,1,0:T(8,128)(2,1)S(1)} async-done(((bf16[8,8,896]{2,1,0:T(8,128)(2,1)}), bf16[8,8,896]{2,1,0:T(8,128)(2,1)S(1)}, u32[]{:S(2)}, u32[]{:S(2)}) %all-to-all-start.1) | async-done | bytes 114720 | tf_op jit(solution)/shard_map/all_to_all | solution.py:56
  92.3 0.6 gather_fusion.1
  92.8 0.8 maximum_convert_fusion
  (25 shorter events, 0.1 us)
Async XLA Ops:
  6.5 4.9 %copy-start = (bf16[8,8,896]{2,1,0:T(8,128)(2,1)S(1)}, bf16[8,8,896]{2,1,0:T(8,128)(2,1)}, u32[]{:S(2)}) copy-start(bf16[8,8,896]{2,1,0:T(8,128)(2,1)} %param.11) | copy-start | bytes 344068
  6.5 3.9 %copy-start.6 = (s32[8]{0:T(128)S(1)}, s32[8]{0:T(128)}, u32[]{:S(2)}) copy-start(s32[8]{0:T(128)} %param.18) | copy-start | bytes 100
  6.5 14.5 %copy-start.1 = (bf16[224,224]{1,0:T(8,128)(2,1)S(1)}, bf16[224,224]{1,0:T(8,128)(2,1)}, u32[]{:S(2)}) copy-start(bf16[224,224]{1,0:T(8,128)(2,1)} %param.13) | copy-start | bytes 301060
  6.5 31.2 %all-gather.7.cloned.1.call-start = ((), (), s32[]{:S(2)}) async-start(), calls=%async_computation.2 | async-start | bytes 2007040 | tf_op jit(solution)/shard_map/all_gather | solution.py:12
  8.9 21.8 %copy-start.2 = (bf16[224,224]{1,0:T(8,128)(2,1)S(1)}, bf16[224,224]{1,0:T(8,128)(2,1)}, u32[]{:S(2)}) copy-start(bf16[224,224]{1,0:T(8,128)(2,1)} %param.14) | copy-start | bytes 301060
  9.0 46.6 %all-gather.9.cloned.1.call-start = ((), (), s32[]{:S(2)}) async-start(), calls=%async_computation.3 | async-start | bytes 2007040 | tf_op jit(solution)/shard_map/all_gather | solution.py:12
  9.7 67.3 %all-gather.11.cloned.1.call-start = ((), (), s32[]{:S(2)}) async-start(), calls=%async_computation.4 | async-start | bytes 2007040 | tf_op jit(solution)/shard_map/all_gather | solution.py:12
  12.8 24.9 %all-to-all-start = ((bf16[8,8,896]{2,1,0:T(8,128)(2,1)}), bf16[8,8,896]{2,1,0:T(8,128)(2,1)S(1)}, u32[]{:S(2)}, u32[]{:S(2)}) async-start(bf16[8,8,896]{2,1,0:T(8,128)(2,1)} %broadcast_select_fusion), calls=%async_computation | async-start | bytes 229376 | tf_op jit(solution)/shard_map/all_to_all | solution.py:48
  58.2 20.6 %copy-start.5 = (f32[896]{0:T(1024)S(1)}, f32[896]{0:T(1024)}, u32[]{:S(2)}) copy-start(f32[896]{0:T(1024)} %param.16) | copy-start | bytes 10756
  58.2 20.6 %copy-start.4 = (f32[896]{0:T(1024)S(1)}, f32[896]{0:T(1024)}, u32[]{:S(2)}) copy-start(f32[896]{0:T(1024)} %param.17) | copy-start | bytes 10756
  58.6 34.2 %copy-start.3 = (bf16[8,8,896]{2,1,0:T(8,128)(2,1)S(1)}, bf16[8,8,896]{2,1,0:T(8,128)(2,1)}, u32[]{:S(2)}) copy-start(bf16[8,8,896]{2,1,0:T(8,128)(2,1)} %param.12) | copy-start | bytes 344068
  79.5 12.8 %all-to-all-start.1 = ((bf16[8,8,896]{2,1,0:T(8,128)(2,1)}), bf16[8,8,896]{2,1,0:T(8,128)(2,1)S(1)}, u32[]{:S(2)}, u32[]{:S(2)}) async-start(bf16[8,8,896]{2,1,0:T(8,128)(2,1)} %add_convert_fusion), calls=%async_computation.1 | async-start | bytes 229376 | tf_op jit(solution)/shard_map/all_to_all | solution.py:56
Sparse Core Ops, SparseCore 0:
  9.1 24.9 all-gather.6
  35.7 19.8 all-gather.8
  57.1 19.8 all-gather.10
where the time goes:
time: 100 us
  waiting for transfers between devices  44.8 us (45%)
  blocking collectives  16.6 us (17%)
  between operations  13.2 us (13%)
  starting transfers between devices  12.9 us (13%)
  matrix products  4.83 us (5%)
  other arithmetic  4.17 us (4%)
  local copies, waits for them, and re-layouts  3.57 us (4%)
    all_gather x3, waiting for transfers between devices, project_rows(): lax.all_gather(weight_rows, 'fsdp', axis=0, tiled=True)  36.2 us
    all_gather x1, blocking collectives, local(): lax.all_gather(se_reduce, 'fsdp', axis=0, tiled=True)  9.71 us
    all_to_all x1, starting transfers between devices, local(): lax.all_to_all(outgoing, 'dp', split_axis=0, concat_axis=0, tiled=True)  7.28 us
    all_to_all x1, waiting for transfers between devices, local(): lax.all_to_all(normed_here, 'dp', split_axis=0, concat_axis=0, tiled=True)  7.23 us
    all_gather x1, blocking collectives, local(): lax.all_gather(se_expand, 'fsdp', axis=0, tiled=True)  6.94 us
    all_to_all x1, starting transfers between devices, local(): lax.all_to_all(normed_here, 'dp', split_axis=0, concat_axis=0, tiled=True)  5.52 us
    dot_general x2, matrix products, project_rows(): jnp.dot(flat, lax.all_gather(weight_rows, 'fsdp', axis=0, tiled=True), pr...  4.4 us
    slice x1, local copies, waits for them, and re-layouts, encode_block(): conv_weight[layer]  2.4 us
  transfers between devices with their start and end apart: 5, of which 3 were waited for; matrix products, arithmetic and copies ran while one was open for 6% of the time, Pallas kernels for 0%

commit v1 on v0

--- a/solution.py
+++ b/solution.py
@@ -1,9 +1,15 @@
+import functools
+
 import jax
 import jax.numpy as jnp
 from jax import lax
+from jax.experimental import pallas as pl
+from jax.experimental.pallas import tpu as pltpu
 from jax.sharding import PartitionSpec as P
 
 epsilon = 1e-05
+lane = 128
+MESH = pl.DeviceIdType.MESH
 
 
 def project_rows(flat, weight_rows):
@@ -35,7 +41,7 @@
     return projected.reshape(images, positions, channels)
 
 
-def local(keys, residual, se_reduce, se_expand, conv_weight, bn_gain, bn_bias, shuffle, unshuffle):
+def local_general(keys, residual, se_reduce, se_expand, conv_weight, bn_gain, bn_bias, shuffle, unshuffle):
     images, positions, channels = keys.shape
     count = images * positions
     reduce_full, expand_full = (
@@ -59,6 +65,298 @@
     return encoded.astype(jnp.bfloat16)
 
 
+def fused_kernel(
+    n_dp,
+    images,
+    positions,
+    keys_ref,
+    reduce_ref,
+    expand_ref,
+    weight_ref,
+    gain_ref,
+    bias_ref,
+    shuffle_ref,
+    out_ref,
+    w,
+    red,
+    exp,
+    kbuf,
+    psend,
+    precv,
+    se_send,
+    se_recv,
+    hbuf,
+    last_send,
+    last_recv,
+    table,
+    sums_recv,
+    stats,
+    stats_recv,
+    key_sem,
+    weight_sem,
+    layer_sem,
+    se_sem,
+    last_sem,
+    sums_send_sem,
+    sums_recv_sem,
+    stats_send_sem,
+    stats_recv_sem,
+):
+    me = lax.axis_index("dp")
+    f = lax.axis_index("fsdp")
+    x, c = f // 2, f % 2
+    sibling = 2 * x + (1 - c)
+    peer = 2 * (1 - x) + c
+    layers, rows_dev, channels = weight_ref.shape
+    half = 2 * rows_dev
+    window = kbuf.shape[2]
+    pad = window - half
+    rows = images * positions
+    own_lo = pl.multiple_of(x * (channels - window), lane)
+    peer_lo = pl.multiple_of((1 - x) * (channels - window), lane)
+    base = pl.multiple_of(x * pad + c * rows_dev, 16)
+
+    keys_own = pltpu.make_async_copy(
+        keys_ref.at[:, pl.ds(own_lo, window)], kbuf.at[x], key_sem.at[0]
+    )
+    keys_own.start()
+    sources = [weight_ref.at[l] for l in range(layers)] + [reduce_ref, expand_ref]
+    targets = [w.at[l] for l in range(layers)] + [red, exp]
+    local_copies = []
+    for s, (src, dst) in enumerate(zip(sources, targets)):
+        copy = pltpu.make_async_copy(src, dst.at[pl.ds(base, rows_dev), :], weight_sem.at[0, s])
+        copy.start()
+        local_copies.append(copy)
+
+    barrier = pltpu.get_barrier_semaphore()
+    for other in (sibling, peer):
+        pl.semaphore_signal(barrier, inc=1, device_id={"fsdp": other}, device_id_type=MESH)
+    for k in range(1, n_dp):
+        pl.semaphore_signal(
+            barrier, inc=1, device_id={"dp": lax.rem(me + k, n_dp)}, device_id_type=MESH
+        )
+    pl.semaphore_wait(barrier, n_dp + 1)
+
+    keys_peer = pltpu.make_async_remote_copy(
+        src_ref=keys_ref.at[:, pl.ds(peer_lo, window)],
+        dst_ref=kbuf.at[x],
+        send_sem=key_sem.at[1],
+        recv_sem=key_sem.at[2],
+        device_id={"fsdp": peer},
+        device_id_type=MESH,
+    )
+    keys_peer.start()
+    shared = {}
+    for s in (0, 1, layers, layers + 1, *range(2, layers)):
+        shared[s] = pltpu.make_async_remote_copy(
+            src_ref=sources[s],
+            dst_ref=targets[s].at[pl.ds(base, rows_dev), :],
+            send_sem=weight_sem.at[1, s],
+            recv_sem=weight_sem.at[2, s],
+            device_id={"fsdp": sibling},
+            device_id_type=MESH,
+        )
+        shared[s].start()
+
+    zero_lo = pl.multiple_of((1 - x) * half, 16)
+    for l in range(layers):
+        w[l, pl.ds(zero_lo, pad), :] = jnp.zeros((pad, channels), w.dtype)
+    red[pl.ds(zero_lo, pad), :] = jnp.zeros((pad, red.shape[1]), red.dtype)
+    exp[pl.ds(zero_lo, pad), :] = jnp.zeros((pad, exp.shape[1]), exp.dtype)
+
+    def have_weights(s):
+        local_copies[s].wait()
+        shared[s].wait_recv()
+
+    def to_peer(src, dst, sems):
+        return pltpu.make_async_remote_copy(
+            src_ref=src,
+            dst_ref=dst,
+            send_sem=sems.at[0],
+            recv_sem=sems.at[1],
+            device_id={"fsdp": peer},
+            device_id_type=MESH,
+        )
+
+    keys_own.wait()
+    keys_peer.wait_recv()
+    pending = []
+    entry = kbuf[...].reshape(2 * rows, window)
+    for l in range(layers - 1):
+        have_weights(l)
+        theirs = jnp.dot(
+            entry, w[l, :, pl.ds(peer_lo, window)], preferred_element_type=jnp.float32
+        )
+        psend[l] = theirs.astype(jnp.bfloat16)
+        copy = to_peer(psend.at[l], precv.at[l], layer_sem.at[l])
+        copy.start()
+        mine = jnp.dot(
+            entry, w[l, :, pl.ds(own_lo, window)], preferred_element_type=jnp.float32
+        )
+        copy.wait_recv()
+        pending.append(copy)
+        entry = jnp.maximum(mine + precv[l].astype(jnp.float32), 0.0).astype(jnp.bfloat16)
+
+    have_weights(layers)
+    have_weights(layers + 1)
+    wide = entry.astype(jnp.float32).reshape(2 * images, positions, window)
+    pooled = (jnp.sum(wide, axis=1) * (1.0 / positions)).astype(jnp.bfloat16)
+    part = jnp.dot(pooled, red[...], preferred_element_type=jnp.float32)
+    se_send[...] = part
+    copy = to_peer(se_send, se_recv, se_sem)
+    copy.start()
+    copy.wait_recv()
+    pending.append(copy)
+    squeeze_act = jnp.maximum(part + se_recv[...], 0.0).astype(jnp.bfloat16)
+    excite = jax.nn.sigmoid(
+        lax.dot_general(
+            squeeze_act, exp[...], (((1,), (1,)), ((), ())), preferred_element_type=jnp.float32
+        )
+    )
+    scaled = (wide * excite[:, None, :]).astype(jnp.bfloat16)
+    hbuf[...] = scaled.reshape(2, rows, window)
+
+    have_weights(layers - 1)
+    theirs = jnp.dot(hbuf[1 - x], w[layers - 1], preferred_element_type=jnp.float32)
+    last_send[...] = theirs.astype(jnp.bfloat16)
+    copy = to_peer(last_send, last_recv, last_sem)
+    copy.start()
+    mine = jnp.dot(hbuf[x], w[layers - 1], preferred_element_type=jnp.float32)
+    copy.wait_recv()
+    pending.append(copy)
+    projected = (mine + last_recv[...].astype(jnp.float32)).reshape(images, positions, channels)
+
+    image_sums = jnp.sum(projected, axis=1)
+    image_squares = jnp.sum(projected * projected, axis=1)
+    dests = [lax.div(shuffle_ref[i], images) for i in range(images)]
+    device_row = lax.broadcasted_iota(jnp.int32, (n_dp, channels), 0)
+    sums_table = jnp.zeros((n_dp, channels), jnp.float32)
+    squares_table = jnp.zeros((n_dp, channels), jnp.float32)
+    for i in range(images):
+        hit = device_row == dests[i]
+        sums_table = sums_table + jnp.where(hit, image_sums[i : i + 1], 0.0)
+        squares_table = squares_table + jnp.where(hit, image_squares[i : i + 1], 0.0)
+    table[:, 0, :] = sums_table
+    table[:, 1, :] = squares_table
+    reduce_copies = []
+    for k in range(1, n_dp):
+        target = lax.rem(me + k, n_dp)
+        copy = pltpu.make_async_remote_copy(
+            src_ref=table.at[target],
+            dst_ref=sums_recv.at[k - 1],
+            send_sem=sums_send_sem.at[k - 1],
+            recv_sem=sums_recv_sem.at[k - 1],
+            device_id={"dp": target},
+            device_id_type=MESH,
+        )
+        copy.start()
+        reduce_copies.append(copy)
+    total = table[me]
+    for k in range(1, n_dp):
+        reduce_copies[k - 1].wait_recv()
+        total = total + sums_recv[k - 1]
+    count = images * positions
+    mean_rows = total[0:1] / count
+    variance = total[1:2] / count - mean_rows * mean_rows
+    stats[0:1, :] = mean_rows
+    stats[1:2, :] = lax.rsqrt(variance + epsilon) * gain_ref[...]
+    gather_copies = []
+    for k in range(1, n_dp):
+        target = lax.rem(me + k, n_dp)
+        copy = pltpu.make_async_remote_copy(
+            src_ref=stats,
+            dst_ref=stats_recv.at[k - 1],
+            send_sem=stats_send_sem.at[k - 1],
+            recv_sem=stats_recv_sem.at[k - 1],
+            device_id={"dp": target},
+            device_id_type=MESH,
+        )
+        copy.start()
+        gather_copies.append(copy)
+
+    image_row = lax.broadcasted_iota(jnp.int32, (images, channels), 0)
+    dest_row = jnp.zeros((images, channels), jnp.int32)
+    for i in range(images):
+        dest_row = jnp.where(image_row == i, dests[i], dest_row)
+    mean_image = jnp.zeros((images, channels), jnp.float32)
+    scale_image = jnp.zeros((images, channels), jnp.float32)
+    for k in range(n_dp):
+        if k == 0:
+            owner, ref = me, stats
+        else:
+            gather_copies[k - 1].wait_recv()
+            owner, ref = lax.rem(me + n_dp - k, n_dp), stats_recv.at[k - 1]
+        hit = dest_row == owner
+        mean_image = jnp.where(hit, ref[0:1, :], mean_image)
+        scale_image = jnp.where(hit, ref[1:2, :], scale_image)
+    normed = (projected - mean_image[:, None, :]) * scale_image[:, None, :] + bias_ref[...][None]
+    out_ref[...] = normed.astype(jnp.bfloat16).reshape(rows, channels)
+
+    keys_peer.wait_send()
+    for s in shared:
+        shared[s].wait_send()
+    for copy in pending + reduce_copies + gather_copies:
+        copy.wait_send()
+
+
+def local_fused(n_dp, keys, residual, se_reduce, se_expand, conv_weight, bn_gain, bn_bias, shuffle, unshuffle):
+    images, positions, channels = keys.shape
+    layers, rows_dev, _ = conv_weight.shape
+    units = se_reduce.shape[1]
+    rows = images * positions
+    half = 2 * rows_dev
+    window = -(-half // lane) * lane
+    bf16, f32 = jnp.bfloat16, jnp.float32
+    vmem = pl.BlockSpec(memory_space=pltpu.VMEM)
+    anywhere = pl.BlockSpec(memory_space=pl.ANY)
+    dma = pltpu.SemaphoreType.DMA
+    normed = pl.pallas_call(
+        functools.partial(fused_kernel, n_dp, images, positions),
+        out_shape=jax.ShapeDtypeStruct((rows, channels), bf16),
+        in_specs=[anywhere] * 4 + [vmem] * 2 + [pl.BlockSpec(memory_space=pltpu.SMEM)],
+        out_specs=vmem,
+        scratch_shapes=[
+            pltpu.VMEM((layers, window, channels), bf16),
+            pltpu.VMEM((window, units), bf16),
+            pltpu.VMEM((window, units), bf16),
+            pltpu.VMEM((2, rows, window), bf16),
+            pltpu.VMEM((layers - 1, 2 * rows, window), bf16),
+            pltpu.VMEM((layers - 1, 2 * rows, window), bf16),
+            pltpu.VMEM((2 * images, units), f32),
+            pltpu.VMEM((2 * images, units), f32),
+            pltpu.VMEM((2, rows, window), bf16),
+            pltpu.VMEM((rows, channels), bf16),
+            pltpu.VMEM((rows, channels), bf16),
+            pltpu.VMEM((n_dp, 2, channels), f32),
+            pltpu.VMEM((n_dp - 1, 2, channels), f32),
+            pltpu.VMEM((2, channels), f32),
+            pltpu.VMEM((n_dp - 1, 2, channels), f32),
+            dma((3,)),
+            dma((3, layers + 2)),
+            dma((layers - 1, 2)),
+            dma((2,)),
+            dma((2,)),
+            dma((n_dp - 1,)),
+            dma((n_dp - 1,)),
+            dma((n_dp - 1,)),
+            dma((n_dp - 1,)),
+        ],
+        compiler_params=pltpu.CompilerParams(collective_id=0, has_side_effects=True),
+        name="fused_encoder",
+    )(
+        keys.reshape(rows, channels),
+        se_reduce,
+        se_expand,
+        conv_weight,
+        bn_gain.reshape(1, channels),
+        bn_bias.reshape(1, channels),
+        shuffle,
+    )
+    normed = normed.reshape(images, positions, channels)
+    encoded = jax.nn.relu(normed.astype(f32) + residual.astype(f32))
+    return encoded.astype(bf16)
+
+
 def solution(mesh):
     placed = (
         P(("dp", "fsdp"), None, None),
@@ -71,6 +369,11 @@
         P(("dp", "fsdp")),
         P(("dp", "fsdp")),
     )
+    n_dp, n_fsdp = mesh.shape["dp"], mesh.shape["fsdp"]
+    if n_fsdp == 4:
+        local = functools.partial(local_fused, n_dp)
+    else:
+        local = local_general
     return jax.shard_map(
         local, mesh=mesh, in_specs=placed, out_specs=P(("dp", "fsdp"), None, None), check_vma=False
     )

time: 100 us -> 41.5 us (0.41)
  waiting for transfers between devices: 44.8 us -> 0 us
  Pallas kernels: 0 us -> 37.1 us
  blocking collectives: 16.6 us -> 0 us
  between operations: 13.2 us -> 0.02 us
  starting transfers between devices: 12.9 us -> 0 us
  matrix products: 4.83 us -> 0 us
  other arithmetic: 4.17 us -> 1.58 us
    pallas_call x0 -> x1, Pallas kernels: none -> 37.1 us  [local_fused(): pl.pallas_call(functools.partial(fused_kernel, n_dp, images, positions),...]
    all_gather x3 -> x0, waiting for transfers between devices: 36.2 us -> none  [project_rows(): lax.all_gather(weight_rows, 'fsdp', axis=0, tiled=True)]
    all_gather x2 -> x0, blocking collectives: 16.6 us -> none  [the longest x1 9.71 us: local(): lax.all_gather(se_reduce, 'fsdp', axis=0, tiled=True)]
    all_to_all x2 -> x0, starting transfers between devices: 12.8 us -> none  [the longest x1 7.28 us: local(): lax.all_to_all(outgoing, 'dp', split_axis=0, concat_axis=0, tiled=True)]
    all_to_all x2 -> x0, waiting for transfers between devices: 7.23 us -> none  [the longest x1 7.23 us: local(): lax.all_to_all(normed_here, 'dp', split_axis=0, concat_axis=0, tiled=True)]
    dot_general x3 -> x0, matrix products: 4.83 us -> none  [the longest x2 4.4 us: project_rows(): jnp.dot(flat, lax.all_gather(weight_rows, 'fsdp', axis=0, tiled=True), pr...]
    reshape x0 -> x2, local copies, waits for them, and re-layouts: none -> 2.58 us  [the longest x1 1.3 us: local_fused(): bn_gain.reshape(1, channels)]
    slice x1 -> x0, local copies, waits for them, and re-layouts: 2.4 us -> none  [encode_block(): conv_weight[layer]]
  transfers between devices with their start and end apart: 5 -> 0, of which waited for: 3 -> 0; matrix products, arithmetic and copies ran while one was open for 6% -> 0% of each run, Pallas kernels for 0% -> 0%
where the time goes in v1:
time: 41.5 us; the launch traced here: 41.3 us
  Pallas kernels  37.1 us (89%)
  local copies, waits for them, and re-layouts  2.58 us (6%)
  other arithmetic  1.58 us (4%)
    pallas_call x1, Pallas kernels, local_fused(): pl.pallas_call(functools.partial(fused_kernel, n_dp, images, positions),...  37.1 us
    convert_element_type x1, other arithmetic, local_fused(): return encoded.astype(bf16)  1.58 us
    reshape x1, local copies, waits for them, and re-layouts, local_fused(): bn_gain.reshape(1, channels)  1.3 us
    reshape x1, local copies, waits for them, and re-layouts, local_fused(): bn_bias.reshape(1, channels)  1.27 us

profile of v1, /device:TPU:0, one launch (start us, length us, event | category | flops | bytes accessed | tf_op | source)
XLA Modules:
  0.0 41.3 jit_solution(8641699710412411447)
XLA Ops:
  0.0 0.0 copy-start
  0.0 1.3 %reshape.13.gain_ref = f32[1,896]{1,0:T(1,128)} reshape(f32[896]{0:T(1024)} %param.14) | data formatting | bytes 7168 | tf_op jit(solution)/shard_map/reshape | solution.py:351
  1.3 1.3 %reshape.14.bias_ref = f32[1,896]{1,0:T(1,128)} reshape(f32[896]{0:T(1024)} %param.15) | data formatting | bytes 7168 | tf_op jit(solution)/shard_map/reshape | solution.py:352
  2.6 37.1 %fused_encoder.1 = bf16[64,896]{1,0:T(8,128)(2,1)} custom-call(bf16[64,896]{1,0:T(8,128)(2,1)} %bitcast.4, bf16[224,224]{1,0:T(8,128)(2,1)} %reduce_ref.1, bf16[224,224]{1,0:T(8,128)(2,1)} %expand_ref.1, bf16[3,224,896]{2,1,0:T(8,128)(2,1)} %weight_ref.1, f32[1,896]{1,0:T(1,128)} %reshape.13.gain_ref, f32[1,896]{1,0:T(1,128)} %reshape.14.bias_ref, s32[8]{0:T(128)} %shuffle_ref.1), custom_call_target="tpu_custom_call" | custom-call | tf_op jit(solution)/shard_map/fused_encoder/pallas_call | solution.py:313
  39.7 0.0 copy-done
  39.7 1.6 %fusion.1 = bf16[8,8,896]{2,1,0:T(8,128)(2,1)} fusion(bf16[8,8,896]{2,1,0:T(8,128)(2,1)S(1)} %copy-done, bf16[64,896]{1,0:T(8,128)(2,1)} %fused_encoder.1), kind=kLoop, calls=%fused_computation.2 | loop fusion | flops 286720 | bytes 344064 | tf_op jit(solution)/shard_map/convert_element_type | solution.py:357
Async XLA Ops:
  0.0 39.7 %copy-start = (bf16[8,8,896]{2,1,0:T(8,128)(2,1)S(1)}, bf16[8,8,896]{2,1,0:T(8,128)(2,1)}, u32[]{:S(2)}) copy-start(bf16[8,8,896]{2,1,0:T(8,128)(2,1)} %param.10) | copy-start | bytes 344068

commit v2 on v1

--- a/solution.py
+++ b/solution.py
@@ -85,7 +85,6 @@
     precv,
     se_send,
     se_recv,
-    hbuf,
     last_send,
     last_recv,
     table,
@@ -101,6 +100,7 @@
     sums_recv_sem,
     stats_send_sem,
     stats_recv_sem,
+    ready_sem,
 ):
     me = lax.axis_index("dp")
     f = lax.axis_index("fsdp")
@@ -128,14 +128,28 @@
         copy.start()
         local_copies.append(copy)
 
+    zero_lo = pl.multiple_of((1 - x) * half, 16)
+    for l in range(layers):
+        w[l, pl.ds(zero_lo, pad), :] = jnp.zeros((pad, channels), w.dtype)
+    red[pl.ds(zero_lo, pad), :] = jnp.zeros((pad, red.shape[1]), red.dtype)
+    exp[pl.ds(zero_lo, pad), :] = jnp.zeros((pad, exp.shape[1]), exp.dtype)
+
     barrier = pltpu.get_barrier_semaphore()
-    for other in (sibling, peer):
-        pl.semaphore_signal(barrier, inc=1, device_id={"fsdp": other}, device_id_type=MESH)
+    pl.semaphore_signal(barrier, inc=1, device_id={"fsdp": peer}, device_id_type=MESH)
     for k in range(1, n_dp):
         pl.semaphore_signal(
             barrier, inc=1, device_id={"dp": lax.rem(me + k, n_dp)}, device_id_type=MESH
         )
-    pl.semaphore_wait(barrier, n_dp + 1)
+
+    @pl.when(c == 0)
+    def _():
+        pl.semaphore_signal(barrier, inc=1, device_id={"fsdp": sibling}, device_id_type=MESH)
+
+    pl.semaphore_wait(barrier, n_dp + c)
+
+    @pl.when(c == 1)
+    def _():
+        pl.semaphore_signal(ready_sem, inc=1, device_id={"fsdp": sibling}, device_id_type=MESH)
 
     keys_peer = pltpu.make_async_remote_copy(
         src_ref=keys_ref.at[:, pl.ds(peer_lo, window)],
@@ -146,6 +160,11 @@
         device_id_type=MESH,
     )
     keys_peer.start()
+
+    @pl.when(c == 0)
+    def _():
+        pl.semaphore_wait(ready_sem, 1)
+
     shared = {}
     for s in (0, 1, layers, layers + 1, *range(2, layers)):
         shared[s] = pltpu.make_async_remote_copy(
@@ -158,18 +177,14 @@
         )
         shared[s].start()
 
-    zero_lo = pl.multiple_of((1 - x) * half, 16)
-    for l in range(layers):
-        w[l, pl.ds(zero_lo, pad), :] = jnp.zeros((pad, channels), w.dtype)
-    red[pl.ds(zero_lo, pad), :] = jnp.zeros((pad, red.shape[1]), red.dtype)
-    exp[pl.ds(zero_lo, pad), :] = jnp.zeros((pad, exp.shape[1]), exp.dtype)
-
     def have_weights(s):
         local_copies[s].wait()
         shared[s].wait_recv()
 
+    pending = []
+
     def to_peer(src, dst, sems):
-        return pltpu.make_async_remote_copy(
+        copy = pltpu.make_async_remote_copy(
             src_ref=src,
             dst_ref=dst,
             send_sem=sems.at[0],
@@ -177,54 +192,73 @@
             device_id={"fsdp": peer},
             device_id_type=MESH,
         )
-
+        copy.start()
+        pending.append(copy)
+        return copy
+
+    chunks = psend.shape[1]
+    part_rows = rows // chunks
+    part_images = 2 * images // chunks
     keys_own.wait()
     keys_peer.wait_recv()
-    pending = []
-    entry = kbuf[...].reshape(2 * rows, window)
+    entries = [
+        kbuf[:, j * part_rows : (j + 1) * part_rows, :].reshape(2 * part_rows, window)
+        for j in range(chunks)
+    ]
+    copies = [None] * chunks
+    mines = [None] * chunks
+
+    def settle(l, j):
+        copies[j].wait_recv()
+        full = mines[j] + precv[l, j].astype(jnp.float32)
+        return jnp.maximum(full, 0.0).astype(jnp.bfloat16)
+
     for l in range(layers - 1):
         have_weights(l)
-        theirs = jnp.dot(
-            entry, w[l, :, pl.ds(peer_lo, window)], preferred_element_type=jnp.float32
-        )
-        psend[l] = theirs.astype(jnp.bfloat16)
-        copy = to_peer(psend.at[l], precv.at[l], layer_sem.at[l])
-        copy.start()
-        mine = jnp.dot(
-            entry, w[l, :, pl.ds(own_lo, window)], preferred_element_type=jnp.float32
-        )
-        copy.wait_recv()
-        pending.append(copy)
-        entry = jnp.maximum(mine + precv[l].astype(jnp.float32), 0.0).astype(jnp.bfloat16)
+        for j in range(chunks):
+            if l > 0:
+                entries[j] = settle(l - 1, j)
+            theirs = jnp.dot(
+                entries[j], w[l, :, pl.ds(peer_lo, window)], preferred_element_type=jnp.float32
+            )
+            psend[l, j] = theirs.astype(jnp.bfloat16)
+            copies[j] = to_peer(psend.at[l, j], precv.at[l, j], layer_sem.at[l, j])
+            mines[j] = jnp.dot(
+                entries[j], w[l, :, pl.ds(own_lo, window)], preferred_element_type=jnp.float32
+            )
 
     have_weights(layers)
     have_weights(layers + 1)
-    wide = entry.astype(jnp.float32).reshape(2 * images, positions, window)
-    pooled = (jnp.sum(wide, axis=1) * (1.0 / positions)).astype(jnp.bfloat16)
-    part = jnp.dot(pooled, red[...], preferred_element_type=jnp.float32)
-    se_send[...] = part
-    copy = to_peer(se_send, se_recv, se_sem)
-    copy.start()
-    copy.wait_recv()
-    pending.append(copy)
-    squeeze_act = jnp.maximum(part + se_recv[...], 0.0).astype(jnp.bfloat16)
-    excite = jax.nn.sigmoid(
-        lax.dot_general(
-            squeeze_act, exp[...], (((1,), (1,)), ((), ())), preferred_element_type=jnp.float32
-        )
-    )
-    scaled = (wide * excite[:, None, :]).astype(jnp.bfloat16)
-    hbuf[...] = scaled.reshape(2, rows, window)
+    wides, parts = [None] * chunks, [None] * chunks
+    for j in range(chunks):
+        entry = settle(layers - 2, j)
+        wides[j] = entry.astype(jnp.float32).reshape(part_images, positions, window)
+        pooled = (jnp.sum(wides[j], axis=1) * (1.0 / positions)).astype(jnp.bfloat16)
+        parts[j] = jnp.dot(pooled, red[...], preferred_element_type=jnp.float32)
+        se_send[j] = parts[j]
+        copies[j] = to_peer(se_send.at[j], se_recv.at[j], se_sem.at[j])
 
     have_weights(layers - 1)
-    theirs = jnp.dot(hbuf[1 - x], w[layers - 1], preferred_element_type=jnp.float32)
-    last_send[...] = theirs.astype(jnp.bfloat16)
-    copy = to_peer(last_send, last_recv, last_sem)
-    copy.start()
-    mine = jnp.dot(hbuf[x], w[layers - 1], preferred_element_type=jnp.float32)
-    copy.wait_recv()
-    pending.append(copy)
-    projected = (mine + last_recv[...].astype(jnp.float32)).reshape(images, positions, channels)
+    for j in range(chunks):
+        copies[j].wait_recv()
+        squeeze_act = jnp.maximum(parts[j] + se_recv[j], 0.0).astype(jnp.bfloat16)
+        excite = jax.nn.sigmoid(
+            lax.dot_general(
+                squeeze_act, exp[...], (((1,), (1,)), ((), ())), preferred_element_type=jnp.float32
+            )
+        )
+        scaled = (wides[j] * excite[:, None, :]).astype(jnp.bfloat16)
+        both = jnp.dot(
+            scaled.reshape(2 * part_rows, window), w[layers - 1], preferred_element_type=jnp.float32
+        )
+        low, high = both[:part_rows], both[part_rows:]
+        last_send[j] = jnp.where(x == 0, high, low).astype(jnp.bfloat16)
+        copies[j] = to_peer(last_send.at[j], last_recv.at[j], last_sem.at[j])
+        mines[j] = jnp.where(x == 0, low, high)
+    for j in range(chunks):
+        copies[j].wait_recv()
+        mines[j] = mines[j] + last_recv[j].astype(jnp.float32)
+    projected = jnp.concatenate(mines, axis=0).reshape(images, positions, channels)
 
     image_sums = jnp.sum(projected, axis=1)
     image_squares = jnp.sum(projected * projected, axis=1)
@@ -259,7 +293,7 @@
     mean_rows = total[0:1] / count
     variance = total[1:2] / count - mean_rows * mean_rows
     stats[0:1, :] = mean_rows
-    stats[1:2, :] = lax.rsqrt(variance + epsilon) * gain_ref[...]
+    stats[1:2, :] = lax.rsqrt(variance + epsilon) * gain_ref[...].reshape(1, channels)
     gather_copies = []
     for k in range(1, n_dp):
         target = lax.rem(me + k, n_dp)
@@ -289,7 +323,7 @@
         hit = dest_row == owner
         mean_image = jnp.where(hit, ref[0:1, :], mean_image)
         scale_image = jnp.where(hit, ref[1:2, :], scale_image)
-    normed = (projected - mean_image[:, None, :]) * scale_image[:, None, :] + bias_ref[...][None]
+    normed = (projected - mean_image[:, None, :]) * scale_image[:, None, :] + bias_ref[...].reshape(1, 1, channels)
     out_ref[...] = normed.astype(jnp.bfloat16).reshape(rows, channels)
 
     keys_peer.wait_send()
@@ -303,6 +337,7 @@
     images, positions, channels = keys.shape
     layers, rows_dev, _ = conv_weight.shape
     units = se_reduce.shape[1]
+    chunks = 2
     rows = images * positions
     half = 2 * rows_dev
     window = -(-half // lane) * lane
@@ -320,26 +355,26 @@
             pltpu.VMEM((window, units), bf16),
             pltpu.VMEM((window, units), bf16),
             pltpu.VMEM((2, rows, window), bf16),
-            pltpu.VMEM((layers - 1, 2 * rows, window), bf16),
-            pltpu.VMEM((layers - 1, 2 * rows, window), bf16),
-            pltpu.VMEM((2 * images, units), f32),
-            pltpu.VMEM((2 * images, units), f32),
-            pltpu.VMEM((2, rows, window), bf16),
-            pltpu.VMEM((rows, channels), bf16),
-            pltpu.VMEM((rows, channels), bf16),
+            pltpu.VMEM((layers - 1, chunks, 2 * rows // chunks, window), bf16),
+            pltpu.VMEM((layers - 1, chunks, 2 * rows // chunks, window), bf16),
+            pltpu.VMEM((chunks, 2 * images // chunks, units), f32),
+            pltpu.VMEM((chunks, 2 * images // chunks, units), f32),
+            pltpu.VMEM((chunks, rows // chunks, channels), bf16),
+            pltpu.VMEM((chunks, rows // chunks, channels), bf16),
             pltpu.VMEM((n_dp, 2, channels), f32),
             pltpu.VMEM((n_dp - 1, 2, channels), f32),
             pltpu.VMEM((2, channels), f32),
             pltpu.VMEM((n_dp - 1, 2, channels), f32),
             dma((3,)),
             dma((3, layers + 2)),
-            dma((layers - 1, 2)),
-            dma((2,)),
-            dma((2,)),
+            dma((layers - 1, chunks, 2)),
+            dma((chunks, 2)),
+            dma((chunks, 2)),
             dma((n_dp - 1,)),
             dma((n_dp - 1,)),
             dma((n_dp - 1,)),
             dma((n_dp - 1,)),
+            pltpu.SemaphoreType.REGULAR,
         ],
         compiler_params=pltpu.CompilerParams(collective_id=0, has_side_effects=True),
         name="fused_encoder",
@@ -348,8 +383,8 @@
         se_reduce,
         se_expand,
         conv_weight,
-        bn_gain.reshape(1, channels),
-        bn_bias.reshape(1, channels),
+        bn_gain,
+        bn_bias,
         shuffle,
     )
     normed = normed.reshape(images, positions, channels)

time: 41.5 us -> 37.8 us (0.911)
  local copies, waits for them, and re-layouts: 2.58 us -> 0.01 us
  Pallas kernels: 37.1 us -> 36 us
    reshape x2 -> x0, local copies, waits for them, and re-layouts: 2.58 us -> none  [the longest x1 1.3 us: local_fused(): bn_gain.reshape(1, channels)]
    pallas_call x1, Pallas kernels: 37.1 us -> 36 us  [local_fused(): pl.pallas_call(functools.partial(fused_kernel, n_dp, images, positions),...]
where the time goes in v2:
time: 37.8 us; the launch traced here: 37.6 us
  Pallas kernels  36 us (95%)
  other arithmetic  1.58 us (4%)
    pallas_call x1, Pallas kernels, local_fused(): pl.pallas_call(functools.partial(fused_kernel, n_dp, images, positions),...  36 us
    convert_element_type x1, other arithmetic, local_fused(): return encoded.astype(bf16)  1.58 us

profile of v2, /device:TPU:0, one launch (start us, length us, event | category | flops | bytes accessed | tf_op | source)
XLA Modules:
  0.0 37.6 jit_solution(10014065818986178233)
XLA Ops:
  0.0 0.0 copy-start
  0.0 36.0 %fused_encoder.1 = bf16[64,896]{1,0:T(8,128)(2,1)} custom-call(bf16[64,896]{1,0:T(8,128)(2,1)} %bitcast.4, bf16[224,224]{1,0:T(8,128)(2,1)} %reduce_ref.1, bf16[224,224]{1,0:T(8,128)(2,1)} %expand_ref.1, bf16[3,224,896]{2,1,0:T(8,128)(2,1)} %weight_ref.1, f32[896]{0:T(1024)} %gain_ref.1, f32[896]{0:T(1024)} %bias_ref.1, s32[8]{0:T(128)} %shuffle_ref.1), custom_call_target="tpu_custom_call" | custom-call | tf_op jit(solution)/shard_map/fused_encoder/pallas_call | solution.py:348
  36.0 0.0 copy-done
  36.1 1.6 %fusion.1 = bf16[8,8,896]{2,1,0:T(8,128)(2,1)} fusion(bf16[8,8,896]{2,1,0:T(8,128)(2,1)S(1)} %copy-done, bf16[64,896]{1,0:T(8,128)(2,1)} %fused_encoder.1), kind=kLoop, calls=%fused_computation.2 | loop fusion | flops 286720 | bytes 344064 | tf_op jit(solution)/shard_map/convert_element_type | solution.py:392
Async XLA Ops:
  0.0 36.0 %copy-start = (bf16[8,8,896]{2,1,0:T(8,128)(2,1)S(1)}, bf16[8,8,896]{2,1,0:T(8,128)(2,1)}, u32[]{:S(2)}) copy-start(bf16[8,8,896]{2,1,0:T(8,128)(2,1)} %param.10) | copy-start | bytes 344068

commit v3 on v2

--- a/solution.py
+++ b/solution.py
@@ -87,19 +87,19 @@
     se_recv,
     last_send,
     last_recv,
-    table,
-    sums_recv,
-    stats,
-    stats_recv,
+    keysv,
+    ksend,
+    nsend,
+    nrecv,
     key_sem,
+    key_send_sem,
+    key_recv_sem,
     weight_sem,
     layer_sem,
     se_sem,
     last_sem,
-    sums_send_sem,
-    sums_recv_sem,
-    stats_send_sem,
-    stats_recv_sem,
+    back_send_sem,
+    back_recv_sem,
     ready_sem,
 ):
     me = lax.axis_index("dp")
@@ -109,17 +109,15 @@
     peer = 2 * (1 - x) + c
     layers, rows_dev, channels = weight_ref.shape
     half = 2 * rows_dev
-    window = kbuf.shape[2]
+    window = kbuf.shape[3]
     pad = window - half
     rows = images * positions
     own_lo = pl.multiple_of(x * (channels - window), lane)
     peer_lo = pl.multiple_of((1 - x) * (channels - window), lane)
     base = pl.multiple_of(x * pad + c * rows_dev, 16)
 
-    keys_own = pltpu.make_async_copy(
-        keys_ref.at[:, pl.ds(own_lo, window)], kbuf.at[x], key_sem.at[0]
-    )
-    keys_own.start()
+    keys_local = pltpu.make_async_copy(keys_ref, keysv, key_sem)
+    keys_local.start()
     sources = [weight_ref.at[l] for l in range(layers)] + [reduce_ref, expand_ref]
     targets = [w.at[l] for l in range(layers)] + [red, exp]
     local_copies = []
@@ -134,32 +132,55 @@
     red[pl.ds(zero_lo, pad), :] = jnp.zeros((pad, red.shape[1]), red.dtype)
     exp[pl.ds(zero_lo, pad), :] = jnp.zeros((pad, exp.shape[1]), exp.dtype)
 
+    dests = [lax.div(shuffle_ref[i], images) for i in range(images)]
+    keys_local.wait()
+    for e in range(n_dp):
+        chosen = jnp.int32(0)
+        for i in range(images):
+            chosen = jnp.where(dests[i] == e, i, chosen)
+        ksend[e] = keysv[chosen]
+
     barrier = pltpu.get_barrier_semaphore()
-    pl.semaphore_signal(barrier, inc=1, device_id={"fsdp": peer}, device_id_type=MESH)
-    for k in range(1, n_dp):
-        pl.semaphore_signal(
-            barrier, inc=1, device_id={"dp": lax.rem(me + k, n_dp)}, device_id_type=MESH
-        )
+    for k in range(n_dp):
+        target = lax.rem(me + k, n_dp)
+        for column in (f, peer):
+            if k > 0 or column is peer:
+                pl.semaphore_signal(
+                    barrier,
+                    inc=1,
+                    device_id={"dp": target, "fsdp": column},
+                    device_id_type=MESH,
+                )
 
     @pl.when(c == 0)
     def _():
         pl.semaphore_signal(barrier, inc=1, device_id={"fsdp": sibling}, device_id_type=MESH)
 
-    pl.semaphore_wait(barrier, n_dp + c)
+    pl.semaphore_wait(barrier, 2 * n_dp - 1 + c)
 
     @pl.when(c == 1)
     def _():
         pl.semaphore_signal(ready_sem, inc=1, device_id={"fsdp": sibling}, device_id_type=MESH)
 
-    keys_peer = pltpu.make_async_remote_copy(
-        src_ref=keys_ref.at[:, pl.ds(peer_lo, window)],
-        dst_ref=kbuf.at[x],
-        send_sem=key_sem.at[1],
-        recv_sem=key_sem.at[2],
-        device_id={"fsdp": peer},
-        device_id_type=MESH,
-    )
-    keys_peer.start()
+    key_copies = []
+    for k in range(n_dp):
+        target = lax.rem(me + k, n_dp)
+        for side, (column, lo) in enumerate(((f, own_lo), (peer, peer_lo))):
+            src = ksend.at[target, :, pl.ds(lo, window)]
+            dst = kbuf.at[x, me]
+            if k == 0 and side == 0:
+                copy = pltpu.make_async_copy(src, dst, key_recv_sem.at[side, k])
+            else:
+                copy = pltpu.make_async_remote_copy(
+                    src_ref=src,
+                    dst_ref=dst,
+                    send_sem=key_send_sem.at[side, k],
+                    recv_sem=key_recv_sem.at[side, k],
+                    device_id={"dp": target, "fsdp": column},
+                    device_id_type=MESH,
+                )
+            copy.start()
+            key_copies.append(copy)
 
     @pl.when(c == 0)
     def _():
@@ -199,10 +220,15 @@
     chunks = psend.shape[1]
     part_rows = rows // chunks
     part_images = 2 * images // chunks
-    keys_own.wait()
-    keys_peer.wait_recv()
+    key_copies[0].wait()
+    for copy in key_copies[1:]:
+        copy.wait_recv()
+    half_images = images // chunks
     entries = [
-        kbuf[:, j * part_rows : (j + 1) * part_rows, :].reshape(2 * part_rows, window)
+        kbuf[:, j * half_images : (j + 1) * half_images]
+        .astype(jnp.float32)
+        .reshape(2 * part_rows, window)
+        .astype(jnp.bfloat16)
         for j in range(chunks)
     ]
     copies = [None] * chunks
@@ -258,78 +284,40 @@
     for j in range(chunks):
         copies[j].wait_recv()
         mines[j] = mines[j] + last_recv[j].astype(jnp.float32)
-    projected = jnp.concatenate(mines, axis=0).reshape(images, positions, channels)
-
-    image_sums = jnp.sum(projected, axis=1)
-    image_squares = jnp.sum(projected * projected, axis=1)
-    dests = [lax.div(shuffle_ref[i], images) for i in range(images)]
-    device_row = lax.broadcasted_iota(jnp.int32, (n_dp, channels), 0)
-    sums_table = jnp.zeros((n_dp, channels), jnp.float32)
-    squares_table = jnp.zeros((n_dp, channels), jnp.float32)
-    for i in range(images):
-        hit = device_row == dests[i]
-        sums_table = sums_table + jnp.where(hit, image_sums[i : i + 1], 0.0)
-        squares_table = squares_table + jnp.where(hit, image_squares[i : i + 1], 0.0)
-    table[:, 0, :] = sums_table
-    table[:, 1, :] = squares_table
-    reduce_copies = []
+    count = images * positions
+    mean_rows = sum(jnp.sum(mine, axis=0, keepdims=True) for mine in mines) / count
+    squares = sum(jnp.sum(mine * mine, axis=0, keepdims=True) for mine in mines) / count
+    scale_rows = lax.rsqrt(squares - mean_rows * mean_rows + epsilon) * gain_ref[...].reshape(
+        1, channels
+    )
+    bias_rows = bias_ref[...].reshape(1, channels)
+    for j in range(chunks):
+        normed = (mines[j] - mean_rows) * scale_rows + bias_rows
+        nsend[j * half_images : (j + 1) * half_images] = normed.reshape(
+            half_images, positions, channels
+        ).astype(jnp.bfloat16)
+
+    back_copies = []
     for k in range(1, n_dp):
         target = lax.rem(me + k, n_dp)
         copy = pltpu.make_async_remote_copy(
-            src_ref=table.at[target],
-            dst_ref=sums_recv.at[k - 1],
-            send_sem=sums_send_sem.at[k - 1],
-            recv_sem=sums_recv_sem.at[k - 1],
+            src_ref=nsend.at[target],
+            dst_ref=nrecv.at[me],
+            send_sem=back_send_sem.at[k - 1],
+            recv_sem=back_recv_sem.at[k - 1],
             device_id={"dp": target},
             device_id_type=MESH,
         )
         copy.start()
-        reduce_copies.append(copy)
-    total = table[me]
-    for k in range(1, n_dp):
-        reduce_copies[k - 1].wait_recv()
-        total = total + sums_recv[k - 1]
-    count = images * positions
-    mean_rows = total[0:1] / count
-    variance = total[1:2] / count - mean_rows * mean_rows
-    stats[0:1, :] = mean_rows
-    stats[1:2, :] = lax.rsqrt(variance + epsilon) * gain_ref[...].reshape(1, channels)
-    gather_copies = []
-    for k in range(1, n_dp):
-        target = lax.rem(me + k, n_dp)
-        copy = pltpu.make_async_remote_copy(
-            src_ref=stats,
-            dst_ref=stats_recv.at[k - 1],
-            send_sem=stats_send_sem.at[k - 1],
-            recv_sem=stats_recv_sem.at[k - 1],
-            device_id={"dp": target},
-            device_id_type=MESH,
-        )
-        copy.start()
-        gather_copies.append(copy)
-
-    image_row = lax.broadcasted_iota(jnp.int32, (images, channels), 0)
-    dest_row = jnp.zeros((images, channels), jnp.int32)
+        back_copies.append(copy)
+    nrecv[me] = nsend[me]
+    for copy in key_copies[1:] + list(shared.values()) + pending:
+        copy.wait_send()
+    for copy in back_copies:
+        copy.wait_recv()
     for i in range(images):
-        dest_row = jnp.where(image_row == i, dests[i], dest_row)
-    mean_image = jnp.zeros((images, channels), jnp.float32)
-    scale_image = jnp.zeros((images, channels), jnp.float32)
-    for k in range(n_dp):
-        if k == 0:
-            owner, ref = me, stats
-        else:
-            gather_copies[k - 1].wait_recv()
-            owner, ref = lax.rem(me + n_dp - k, n_dp), stats_recv.at[k - 1]
-        hit = dest_row == owner
-        mean_image = jnp.where(hit, ref[0:1, :], mean_image)
-        scale_image = jnp.where(hit, ref[1:2, :], scale_image)
-    normed = (projected - mean_image[:, None, :]) * scale_image[:, None, :] + bias_ref[...].reshape(1, 1, channels)
-    out_ref[...] = normed.astype(jnp.bfloat16).reshape(rows, channels)
-
-    keys_peer.wait_send()
-    for s in shared:
-        shared[s].wait_send()
-    for copy in pending + reduce_copies + gather_copies:
+        out_ref[i] = nrecv[dests[i]]
+    for copy in back_copies:
         copy.wait_send()
 
 
@@ -347,31 +335,31 @@
     dma = pltpu.SemaphoreType.DMA
     normed = pl.pallas_call(
         functools.partial(fused_kernel, n_dp, images, positions),
-        out_shape=jax.ShapeDtypeStruct((rows, channels), bf16),
+        out_shape=jax.ShapeDtypeStruct((images, positions, channels), bf16),
         in_specs=[anywhere] * 4 + [vmem] * 2 + [pl.BlockSpec(memory_space=pltpu.SMEM)],
         out_specs=vmem,
         scratch_shapes=[
             pltpu.VMEM((layers, window, channels), bf16),
             pltpu.VMEM((window, units), bf16),
             pltpu.VMEM((window, units), bf16),
-            pltpu.VMEM((2, rows, window), bf16),
+            pltpu.VMEM((2, images, positions, window), bf16),
             pltpu.VMEM((layers - 1, chunks, 2 * rows // chunks, window), bf16),
             pltpu.VMEM((layers - 1, chunks, 2 * rows // chunks, window), bf16),
             pltpu.VMEM((chunks, 2 * images // chunks, units), f32),
             pltpu.VMEM((chunks, 2 * images // chunks, units), f32),
             pltpu.VMEM((chunks, rows // chunks, channels), bf16),
             pltpu.VMEM((chunks, rows // chunks, channels), bf16),
-            pltpu.VMEM((n_dp, 2, channels), f32),
-            pltpu.VMEM((n_dp - 1, 2, channels), f32),
-            pltpu.VMEM((2, channels), f32),
-            pltpu.VMEM((n_dp - 1, 2, channels), f32),
-            dma((3,)),
+            pltpu.VMEM((images, positions, channels), bf16),
+            pltpu.VMEM((n_dp, positions, channels), bf16),
+            pltpu.VMEM((images, positions, channels), bf16),
+            pltpu.VMEM((n_dp, positions, channels), bf16),
+            dma,
+            dma((2, n_dp)),
+            dma((2, n_dp)),
             dma((3, layers + 2)),
             dma((layers - 1, chunks, 2)),
             dma((chunks, 2)),
             dma((chunks, 2)),
-            dma((n_dp - 1,)),
-            dma((n_dp - 1,)),
             dma((n_dp - 1,)),
             dma((n_dp - 1,)),
             pltpu.SemaphoreType.REGULAR,
@@ -379,7 +367,7 @@
         compiler_params=pltpu.CompilerParams(collective_id=0, has_side_effects=True),
         name="fused_encoder",
     )(
-        keys.reshape(rows, channels),
+        keys,
         se_reduce,
         se_expand,
         conv_weight,
@@ -387,7 +375,6 @@
         bn_bias,
         shuffle,
     )
-    normed = normed.reshape(images, positions, channels)
     encoded = jax.nn.relu(normed.astype(f32) + residual.astype(f32))
     return encoded.astype(bf16)
 
@@ -405,10 +392,12 @@
         P(("dp", "fsdp")),
     )
     n_dp, n_fsdp = mesh.shape["dp"], mesh.shape["fsdp"]
-    if n_fsdp == 4:
-        local = functools.partial(local_fused, n_dp)
-    else:
-        local = local_general
+
+    def local(keys, *others):
+        if n_fsdp == 4 and keys.shape[0] == n_dp:
+            return local_fused(n_dp, keys, *others)
+        return local_general(keys, *others)
+
     return jax.shard_map(
         local, mesh=mesh, in_specs=placed, out_specs=P(("dp", "fsdp"), None, None), check_vma=False
     )

time: 37.8 us -> 35.9 us (0.950)
  Pallas kernels: 36 us -> 34.1 us
    pallas_call x1, Pallas kernels: 36 us -> 34.1 us  [local_fused(): pl.pallas_call(functools.partial(fused_kernel, n_dp, images, positions),...]
where the time goes in v3:
time: 35.9 us; the launch traced here: 35.7 us
  Pallas kernels  34.1 us (95%)
  other arithmetic  1.58 us (4%)
    pallas_call x1, Pallas kernels, local_fused(): pl.pallas_call(functools.partial(fused_kernel, n_dp, images, positions),...  34.1 us
    convert_element_type x1, other arithmetic, local_fused(): return encoded.astype(bf16)  1.58 us

profile of v3, /device:TPU:0, one launch (start us, length us, event | category | flops | bytes accessed | tf_op | source)
XLA Modules:
  0.0 35.7 jit_solution(4282036593705656857)
XLA Ops:
  0.0 0.0 copy-start
  0.0 34.1 %fused_encoder.1 = bf16[8,8,896]{2,1,0:T(8,128)(2,1)} custom-call(bf16[8,8,896]{2,1,0:T(8,128)(2,1)} %keys_ref.1, bf16[224,224]{1,0:T(8,128)(2,1)} %reduce_ref.1, bf16[224,224]{1,0:T(8,128)(2,1)} %expand_ref.1, bf16[3,224,896]{2,1,0:T(8,128)(2,1)} %weight_ref.1, f32[896]{0:T(1024)} %gain_ref.1, f32[896]{0:T(1024)} %bias_ref.1, s32[8]{0:T(128)} %shuffle_ref.1), custom_call_target="tpu_custom_call" | custom-call | tf_op jit(solution)/shard_map/fused_encoder/pallas_call | solution.py:336
  34.1 0.0 copy-done
  34.1 1.6 %maximum_convert_fusion = bf16[8,8,896]{2,1,0:T(8,128)(2,1)} fusion(bf16[8,8,896]{2,1,0:T(8,128)(2,1)S(1)} %copy-done, bf16[8,8,896]{2,1,0:T(8,128)(2,1)} %fused_encoder.1), kind=kLoop, calls=%fused_computation | loop fusion | flops 286720 | bytes 344064 | tf_op jit(solution)/shard_map/convert_element_type | solution.py:379
Async XLA Ops:
  0.0 34.1 %copy-start = (bf16[8,8,896]{2,1,0:T(8,128)(2,1)S(1)}, bf16[8,8,896]{2,1,0:T(8,128)(2,1)}, u32[]{:S(2)}) copy-start(bf16[8,8,896]{2,1,0:T(8,128)(2,1)} %param.10) | copy-start | bytes 344068

commit v4 on v3

--- a/solution.py
+++ b/solution.py
@@ -311,13 +311,11 @@
         copy.start()
         back_copies.append(copy)
     nrecv[me] = nsend[me]
-    for copy in key_copies[1:] + list(shared.values()) + pending:
-        copy.wait_send()
     for copy in back_copies:
         copy.wait_recv()
     for i in range(images):
         out_ref[i] = nrecv[dests[i]]
-    for copy in back_copies:
+    for copy in key_copies[1:] + list(shared.values()) + pending + back_copies:
         copy.wait_send()
 
 
@@ -325,7 +323,7 @@
     images, positions, channels = keys.shape
     layers, rows_dev, _ = conv_weight.shape
     units = se_reduce.shape[1]
-    chunks = 2
+    chunks = 4
     rows = images * positions
     half = 2 * rows_dev
     window = -(-half // lane) * lane

time: 35.9 us -> 35.7 us (level)
  no operation moved by 1% of the time
where the time goes in v4:
time: 35.7 us; the launch traced here: 35.5 us
  Pallas kernels  33.9 us (95%)
  other arithmetic  1.58 us (4%)
    pallas_call x1, Pallas kernels, local_fused(): pl.pallas_call(functools.partial(fused_kernel, n_dp, images, positions),...  33.9 us
    convert_element_type x1, other arithmetic, local_fused(): return encoded.astype(bf16)  1.58 us

profile of v4, /device:TPU:0, one launch (start us, length us, event | category | flops | bytes accessed | tf_op | source)
XLA Modules:
  0.0 35.5 jit_solution(5788081956962935286)
XLA Ops:
  0.0 0.0 copy-start
  0.0 33.9 %fused_encoder.1 = bf16[8,8,896]{2,1,0:T(8,128)(2,1)} custom-call(bf16[8,8,896]{2,1,0:T(8,128)(2,1)} %keys_ref.1, bf16[224,224]{1,0:T(8,128)(2,1)} %reduce_ref.1, bf16[224,224]{1,0:T(8,128)(2,1)} %expand_ref.1, bf16[3,224,896]{2,1,0:T(8,128)(2,1)} %weight_ref.1, f32[896]{0:T(1024)} %gain_ref.1, f32[896]{0:T(1024)} %bias_ref.1, s32[8]{0:T(128)} %shuffle_ref.1), custom_call_target="tpu_custom_call" | custom-call | tf_op jit(solution)/shard_map/fused_encoder/pallas_call | solution.py:334
  34.0 0.0 copy-done
  34.0 1.6 %maximum_convert_fusion = bf16[8,8,896]{2,1,0:T(8,128)(2,1)} fusion(bf16[8,8,896]{2,1,0:T(8,128)(2,1)S(1)} %copy-done, bf16[8,8,896]{2,1,0:T(8,128)(2,1)} %fused_encoder.1), kind=kLoop, calls=%fused_computation | loop fusion | flops 286720 | bytes 344064 | tf_op jit(solution)/shard_map/convert_element_type | solution.py:377
Async XLA Ops:
  0.0 34.0 %copy-start = (bf16[8,8,896]{2,1,0:T(8,128)(2,1)S(1)}, bf16[8,8,896]{2,1,0:T(8,128)(2,1)}, u32[]{:S(2)}) copy-start(bf16[8,8,896]{2,1,0:T(8,128)(2,1)} %param.10) | copy-start | bytes 344068

commit v5 on v4

--- a/solution.py
+++ b/solution.py
@@ -239,6 +239,11 @@
         full = mines[j] + precv[l, j].astype(jnp.float32)
         return jnp.maximum(full, 0.0).astype(jnp.bfloat16)
 
+    def own_part(l, j):
+        return jnp.dot(
+            entries[j], w[l, :, pl.ds(own_lo, window)], preferred_element_type=jnp.float32
+        )
+
     for l in range(layers - 1):
         have_weights(l)
         for j in range(chunks):
@@ -249,9 +254,10 @@
             )
             psend[l, j] = theirs.astype(jnp.bfloat16)
             copies[j] = to_peer(psend.at[l, j], precv.at[l, j], layer_sem.at[l, j])
-            mines[j] = jnp.dot(
-                entries[j], w[l, :, pl.ds(own_lo, window)], preferred_element_type=jnp.float32
-            )
+            if l > 0:
+                mines[j] = own_part(l, j)
+        if l == 0:
+            mines = [own_part(l, j) for j in range(chunks)]
 
     have_weights(layers)
     have_weights(layers + 1)

time: 35.7 us -> 35.7 us (level)
  no operation moved by 1% of the time
where the time goes in v5:
time: 35.7 us; the launch traced here: 35.5 us
  Pallas kernels  33.9 us (95%)
  other arithmetic  1.58 us (4%)
    pallas_call x1, Pallas kernels, local_fused(): pl.pallas_call(functools.partial(fused_kernel, n_dp, images, positions),...  33.9 us
    convert_element_type x1, other arithmetic, local_fused(): return encoded.astype(bf16)  1.58 us

profile of v5, /device:TPU:0, one launch (start us, length us, event | category | flops | bytes accessed | tf_op | source)
XLA Modules:
  0.0 35.5 jit_solution(18312290963087887356)
XLA Ops:
  0.0 0.0 copy-start
  0.0 33.9 %fused_encoder.1 = bf16[8,8,896]{2,1,0:T(8,128)(2,1)} custom-call(bf16[8,8,896]{2,1,0:T(8,128)(2,1)} %keys_ref.1, bf16[224,224]{1,0:T(8,128)(2,1)} %reduce_ref.1, bf16[224,224]{1,0:T(8,128)(2,1)} %expand_ref.1, bf16[3,224,896]{2,1,0:T(8,128)(2,1)} %weight_ref.1, f32[896]{0:T(1024)} %gain_ref.1, f32[896]{0:T(1024)} %bias_ref.1, s32[8]{0:T(128)} %shuffle_ref.1), custom_call_target="tpu_custom_call" | custom-call | tf_op jit(solution)/shard_map/fused_encoder/pallas_call | solution.py:340
  34.0 0.0 copy-done
  34.0 1.6 %maximum_convert_fusion = bf16[8,8,896]{2,1,0:T(8,128)(2,1)} fusion(bf16[8,8,896]{2,1,0:T(8,128)(2,1)S(1)} %copy-done, bf16[8,8,896]{2,1,0:T(8,128)(2,1)} %fused_encoder.1), kind=kLoop, calls=%fused_computation | loop fusion | flops 286720 | bytes 344064 | tf_op jit(solution)/shard_map/convert_element_type | solution.py:383
Async XLA Ops:
  0.0 34.0 %copy-start = (bf16[8,8,896]{2,1,0:T(8,128)(2,1)S(1)}, bf16[8,8,896]{2,1,0:T(8,128)(2,1)}, u32[]{:S(2)}) copy-start(bf16[8,8,896]{2,1,0:T(8,128)(2,1)} %param.10) | copy-start | bytes 344068
